TPU v7x, 32 devices: a whole 2x2x4 slice. The times are simulated.
32 devices in a mesh: dp: 8 (over z, core), mp: 4 (over y, x).
Axes of the slice: x: 2, y: 2, z: 4, core: 2. Of those that a mesh axis runs over, the one named last changes fastest.
Arguments:
- tokens: bfloat16 [65536, 1024], P('dp'), may hold values from -7 to 7
- segments: int32 [64, 1024], P('dp'), may hold values from 0 to 3, never falling along the last dimension, each value on 1 to 512 neighbouring positions
- routes: int32 [64, 128], P('dp'), may hold values from 0 to 1023, as said below
- cotangent: bfloat16 [65536, 1024], P('dp'), may hold values from -6 to 6
- gain_attn: bfloat16 [1024], replicated, may hold values from 0.5 to 1.5
- gain_mlp: bfloat16 [1024], replicated, may hold values from 0.5 to 1.5
- w_router: bfloat16 [1024], replicated, may hold values from -1 to 1
- w_qkv: bfloat16 [1024, 3072], P(None, 'mp'), may hold values from -0.1875 to 0.1875
- w_out: bfloat16 [1024, 1024], P('mp'), may hold values from -0.75 to 0.75
- w_up: bfloat16 [1024, 4096], P(None, 'mp'), may hold values from -0.1875 to 0.1875
- w_down: bfloat16 [4096, 1024], P('mp'), may hold values from -0.09375 to 0.09375
Outputs:
- output: bfloat16 [65536, 1024], P('dp')
- grad_tokens: bfloat16 [65536, 1024], P('dp')
- grad_gain_attn: float32 [1024], replicated
- grad_gain_mlp: float32 [1024], replicated
- grad_router: float32 [1024], replicated
- grad_qkv: float32 [1024, 3072], P(None, 'mp')
- grad_out: float32 [1024, 1024], P('mp')
- grad_up: float32 [1024, 4096], P(None, 'mp')
- grad_down: float32 [4096, 1024], P('mp')
- routed_share: float32 [], replicated
- mean_score: float32 [], replicated
Inputs may be any that keep to these rules, and one draw needn't show every extreme that they name: `routes`: each row holds 128 different positions of its sequence in ascending order, the first 0 and the last 1023. The segment numbers of one sequence never fall; each of the 4 segments has 1 to 512 positions, one exactly 512.
All inputs are finite; a program needn't handle non-finite values.
Results may differ from a plain program's by a relative error of at most 0.012.
Values may be sent and summed in bfloat16 or wider, within the bound.
No kernel may reach another device: no remote copies, remote signals or barrier semaphores. Data moves between devices by JAX's collectives and lax.ppermute only.
A program may use at most 256 MiB of HBM per device.

v0:
```python
import jax
import jax.numpy as jnp
from jax import lax
from jax.sharding import PartitionSpec as P

HD = 64


def rms_scale(inputs, gain_vec):
    inverse = lax.rsqrt(jnp.mean(inputs * inputs, axis=-1, keepdims=True) + 1e-06)
    return inputs * inverse * gain_vec


def transposed(left, right):
    return lax.dot_general(
        left, right, (((0,), (0,)), ((), ())), preferred_element_type=jnp.float32
    )


def shards(
    tokens, segments, routes, cotangent, gain_attn, gain_mlp, w_router, w_qkv, w_out, w_up, w_down
):
    seq_count, seq_len = segments.shape
    routed = routes.shape[1]
    local_heads = w_out.shape[0] // HD
    scale = HD ** (-0.5)
    row_total = seq_count * routed
    offsets = lax.broadcasted_iota(jnp.int32, (seq_count, routed), 0) * seq_len
    picks = (routes + offsets).reshape(-1)
    logits = jnp.dot(tokens, w_router, preferred_element_type=jnp.float32)
    scores = jax.nn.sigmoid(logits)
    rate_routed = scores[picks]
    routed_local = jnp.sum(rate_routed)
    score_local = jnp.sum(scores)
    routed_total, score_total = lax.psum((routed_local, score_local), "dp")
    rows_routed = tokens[picks].astype(jnp.float32)
    grad_rows = cotangent[picks].astype(jnp.float32)
    seg_routed = segments.reshape(-1)[picks].reshape(seq_count, routed)
    gain_one = gain_attn.astype(jnp.float32)
    gain_two = gain_mlp.astype(jnp.float32)
    router_vec = w_router.astype(jnp.float32)
    normed_one = rms_scale(rows_routed, gain_one).astype(jnp.bfloat16)
    joint_qkv = jnp.dot(normed_one, w_qkv, preferred_element_type=jnp.float32).astype(jnp.bfloat16)
    joint_qkv = joint_qkv.reshape(seq_count, routed, local_heads, 3, HD)
    queries = joint_qkv[:, :, :, 0]
    key_rows = joint_qkv[:, :, :, 1]
    values = joint_qkv[:, :, :, 2]
    causal = lax.broadcasted_iota(jnp.int32, (routed, routed), 0) >= lax.broadcasted_iota(
        jnp.int32, (routed, routed), 1
    )
    allowed = causal[None, None] & (seg_routed[:, None, :, None] == seg_routed[:, None, None, :])

    def masked_scores():
        raw_scores = (
            jnp.einsum("sqhe,skhe->shqk", queries, key_rows, preferred_element_type=jnp.float32)
            * scale
        )
        return jnp.where(allowed, raw_scores, -1e30)

    masked = masked_scores()
    top_score = jnp.max(masked, axis=-1, keepdims=True)
    expon_terms = jnp.exp(masked - top_score)
    totals = jnp.sum(expon_terms, axis=-1, keepdims=True)
    probs = expon_terms / totals
    log_total = top_score + jnp.log(totals)
    mixed = jnp.einsum(
        "shqk,skhe->sqhe", probs.astype(jnp.bfloat16), values, preferred_element_type=jnp.float32
    )
    heads_out = mixed.astype(jnp.bfloat16).reshape(row_total, local_heads * HD)
    rate_col = rate_routed[:, None]
    attended = lax.psum(jnp.dot(heads_out, w_out, preferred_element_type=jnp.float32), "mp")
    middle = rows_routed + attended
    normed_two = rms_scale(middle, gain_two).astype(jnp.bfloat16)
    pre_act = jnp.dot(normed_two, w_up, preferred_element_type=jnp.float32)
    hidden = jax.nn.gelu(pre_act).astype(jnp.bfloat16)
    mlp_out = lax.psum(jnp.dot(hidden, w_down, preferred_element_type=jnp.float32), "mp")
    delta_rows = attended + mlp_out
    updated_low = (rows_routed + rate_col * delta_rows).astype(jnp.bfloat16)
    router_term = jnp.sum(grad_rows * delta_rows, axis=-1) * rate_routed * (1.0 - rate_routed)
    output = tokens.at[picks].set(updated_low)
    grad_mlp_out = (rate_col * grad_rows).astype(jnp.bfloat16)
    grad_down = transposed(hidden, grad_mlp_out)
    grad_hidden = jnp.dot(grad_mlp_out, w_down.T, preferred_element_type=jnp.float32)
    unused, gelu_pull = jax.vjp(jax.nn.gelu, pre_act)
    grad_pre = gelu_pull(grad_hidden)[0].astype(jnp.bfloat16)
    grad_up = transposed(normed_two, grad_pre)
    grad_normed_two = lax.psum(jnp.dot(grad_pre, w_up.T, preferred_element_type=jnp.float32), "mp")
    unused, second_pull = jax.vjp(rms_scale, middle, gain_two)
    grad_middle, grad_gain_mlp = second_pull(grad_normed_two)
    grad_attended = (rate_col * grad_rows + grad_middle).astype(jnp.bfloat16)
    grad_out = transposed(heads_out, grad_attended)
    grad_mixed = jnp.dot(grad_attended, w_out.T, preferred_element_type=jnp.float32).astype(
        jnp.bfloat16
    )
    grad_mixed = grad_mixed.reshape(seq_count, routed, local_heads, HD)
    again = masked_scores()
    probs_again = jnp.exp(again - log_total)
    probs_low = probs_again.astype(jnp.bfloat16)
    grad_values = jnp.einsum(
        "shqk,sqhe->skhe", probs_low, grad_mixed, preferred_element_type=jnp.float32
    )
    grad_probs = jnp.einsum(
        "sqhe,skhe->shqk", grad_mixed, values, preferred_element_type=jnp.float32
    )
    row_dots = jnp.sum(probs_again * grad_probs, axis=-1, keepdims=True)
    grad_logits = (probs_again * (grad_probs - row_dots)).astype(jnp.bfloat16)
    grad_queries = (
        jnp.einsum("shqk,skhe->sqhe", grad_logits, key_rows, preferred_element_type=jnp.float32)
        * scale
    )
    grad_keys = (
        jnp.einsum("shqk,sqhe->skhe", grad_logits, queries, preferred_element_type=jnp.float32)
        * scale
    )
    grad_joint = jnp.stack([grad_queries, grad_keys, grad_values], axis=3).astype(jnp.bfloat16)
    grad_joint = grad_joint.reshape(row_total, local_heads * 3 * HD)
    grad_qkv = transposed(normed_one, grad_joint)
    grad_normed_one = lax.psum(
        jnp.dot(grad_joint, w_qkv.T, preferred_element_type=jnp.float32), "mp"
    )
    unused, first_pull = jax.vjp(rms_scale, rows_routed, gain_one)
    grad_first, grad_gain_attn = first_pull(grad_normed_one)
    grad_router = jnp.sum(router_term[:, None] * rows_routed, axis=0)
    grad_routed_rows = (
        grad_rows + grad_middle + grad_first + router_term[:, None] * router_vec[None, :]
    )
    grad_rows_low = grad_routed_rows.astype(jnp.bfloat16)
    grad_tokens = cotangent.at[picks].set(grad_rows_low)
    grad_gain_attn, grad_gain_mlp, grad_router, grad_qkv, grad_out, grad_up, grad_down = lax.psum(
        (grad_gain_attn, grad_gain_mlp, grad_router, grad_qkv, grad_out, grad_up, grad_down), "dp"
    )
    token_count = seq_count * seq_len * lax.axis_size("dp")
    routed_share = routed_total / score_total
    mean_score = score_total / token_count
    return (
        output,
        grad_tokens,
        grad_gain_attn,
        grad_gain_mlp,
        grad_router,
        grad_qkv,
        grad_out,
        grad_up,
        grad_down,
        routed_share,
        mean_score,
    )


def solution(mesh):
    in_specs = (
        P("dp", None),
        P("dp", None),
        P("dp", None),
        P("dp", None),
        P(),
        P(),
        P(),
        P(None, "mp"),
        P("mp", None),
        P(None, "mp"),
        P("mp", None),
    )
    out_specs = (
        P("dp", None),
        P("dp", None),
        P(),
        P(),
        P(),
        P(None, "mp"),
        P("mp", None),
        P(None, "mp"),
        P("mp", None),
        P(),
        P(),
    )
    return jax.shard_map(shards, mesh=mesh, in_specs=in_specs, out_specs=out_specs, check_vma=False)
```

profile of v0, /device:TPU:0, one launch (start us, length us, event | category | flops | bytes accessed | tf_op | source)
XLA Modules:
  0.0 775.4 jit_solution(11880056417674116861)
XLA Ops:
  7.3 14.9 %copy.102 = bf16[8192,1024]{1,0:T(8,128)(2,1)} copy(bf16[8192,1024]{1,0:T(8,128)(2,1)} %param.11) | data formatting | bytes 33554432
  22.2 2.1 copy-done.11
  24.3 6.2 copy.103
  30.5 13.9 %gather_fusion = bf16[1024,1024]{1,0:T(8,128)(2,1)} fusion(bf16[8192,1024]{1,0:T(8,128)(2,1)} %copy.102, s32[1024]{0:T(1024)S(1)} %broadcast_clamp_fusion), kind=kCustom, calls=%fused_computation | custom fusion | bytes 4198400 | tf_op jit(solution)/shard_map/gather | solution.py:36
  44.5 2.1 fusion.18
  46.6 5.0 convolution_convert_fusion
  51.6 2.6 copy.31
  54.2 1.8 copy.53
  57.0 6.2 gather_fusion.2
  63.4 1.6 fusion.65
  66.8 2.8 fusion.52
  70.3 10.2 %fusion.66 = f32[1,8192]{1,0:T(1,128)S(1)} fusion(bf16[8192,1024]{1,0:T(8,128)(2,1)} %copy.102, bf16[1024,1]{0,1:T(2,128)(2,1)S(1)} %reshape.200), kind=kOutput, calls=%fused_computation.113 | convolution fusion | flops 16777216 | bytes 16812032 | tf_op jit(solution)/shard_map/dot_general | solution.py:30
  81.1 6.1 gather_fusion.1
  87.3 14.4 %gather_fusion.3 = bf16[1024,1024]{1,0:T(8,128)(2,1)} fusion(bf16[8192,1024]{1,0:T(8,128)(2,1)} %copy.103, s32[1024]{0:T(1024)S(1)} %broadcast_clamp_fusion), kind=kCustom, calls=%fused_computation.3 | custom fusion | bytes 4198400 | tf_op jit(solution)/shard_map/gather | solution.py:37
  101.6 74.5 %all-reduce.8.cloned.1.call-done = f32[1024,1024]{1,0:T(8,128)} async-done(((f32[1024,1024]{1,0:T(8,128)}), f32[1024,1024]{1,0:T(8,128)}) %all-reduce.8.cloned.1.call-update) | async-done | bytes 4194320 | tf_op jit(solution)/shard_map/psum | solution.py:71
  176.1 3.5 multiply_reduce_fusion.2
  179.6 2.4 fusion.60
  183.3 5.2 fusion.13
  188.6 1.3 copy-done.34
  189.9 4.3 fusion.67
  194.7 7.6 fusion.61
  202.4 95.7 %all-reduce.10.cloned.1.call-done = f32[1024,1024]{1,0:T(8,128)} async-done(((f32[1024,1024]{1,0:T(8,128)}), f32[1024,1024]{1,0:T(8,128)}) %all-reduce.10.cloned.1.call-update) | async-done | bytes 4194320 | tf_op jit(solution)/shard_map/psum | solution.py:87
  298.0 4.6 multiply_reduce_fusion
  302.7 1.3 copy-done.5
  303.9 1.5 fusion.6
  305.5 1.3 copy-done.13
  306.8 1.6 convolution_convert_fusion.2
  308.4 2.8 reshape.202
  311.2 1.5 copy.38
  312.7 1.8 multiply_reduce_fusion.3
  319.8 3.9 fusion.30
  323.9 1.3 copy-done.35
  325.2 6.8 fusion.59
  332.1 5.1 fusion.42
  337.2 1.7 fusion.50
  338.9 3.7 fusion.28
  342.7 153.2 %all-reduce.14.cloned.1.call-done = (f32[1024,1024]{1,0:T(8,128)}, f32[1024,1024]{1,0:T(8,128)}) async-done(((f32[1024,1024]{1,0:T(8,128)}, f32[1024,1024]{1,0:T(8,128)}), (f32[1024,1024]{1,0:T(8,128)}, f32[1024,1024]{1,0:T(8,128)})) %all-reduce.14.cloned.1.call-update) | async-done | bytes 8388624 | tf_op jit(solution)/shard_map/psum | solution.py:76
  495.9 4.8 fusion.17
  501.3 1.9 fusion.5
  503.2 31.0 %all-reduce = (f32[1024]{0:T(1024)}, f32[1024]{0:T(1024)}, f32[1024]{0:T(1024)}, f32[]{:T(128)}, f32[]{:T(128)}) all-reduce(f32[1024]{0:T(1024)S(1)} %get-tuple-element.13, f32[1024]{0:T(1024)S(1)} %get-tuple-element.11, f32[1024]{0:T(1024)S(1)} %get-tuple-element.15, f32[]{:T(128)} %get-tuple-element.34, ...), channel_id=1, replica_groups=mesh['dp'=8,'mp'=4] {'dp'}, use_global_device_ids=true, to_apply=%region_15.16 | all-reduce | flops 3074 | bytes 24592 | tf_op jit(solution)/shard_map/psum | solution.py:129
  536.2 7.6 fusion.16
  543.9 21.8 %scatter_fusion = bf16[8192,1024]{1,0:T(8,128)(2,1)} fusion(bf16[8192,1024]{1,0:T(8,128)(2,1)} %copy.103, s32[1024]{0:T(1024)S(1)} %bitcast.98, bf16[1024,1024]{1,0:T(8,128)(2,1)} %fusion.16), kind=kCustom, calls=%fused_computation.5 | custom fusion | bytes 6295552 | tf_op jit(solution)/shard_map/scatter | solution.py:128
  565.7 23.0 %scatter_custom_fusion = bf16[8192,1024]{1,0:T(8,128)(2,1)} fusion(bf16[8192,1024]{1,0:T(8,128)(2,1)} %copy.102, s32[1024]{0:T(1024)S(1)} %bitcast.99, bf16[1024,1024]{1,0:T(8,128)(2,1)S(1)} %copy-done.2, f32[1024]{0:T(1024)S(1)} %gather_fusion.1, f32[1024,1024]{1,0:T(8,128)} %all-reduce.8.cloned.1.call-done, f32[1024,1024]{1,0:T(8,128)} %get-tuple-element.25), kind=kCustom, calls=%fused_computation.47 | custom fusion | flops 5242880 | bytes 27267072 | tf_op jit(solution)/shard_map/scatter | solution.py:80
  588.6 166.8 %all-reduce.12.cloned.1.call-done = (f32[1024,768]{1,0:T(8,128)}, f32[256,1024]{1,0:T(8,128)}, f32[1024,1024]{1,0:T(8,128)}, f32[1024,1024]{1,0:T(8,128)}) async-done(((f32[1024,768]{1,0:T(8,128)}, f32[256,1024]{1,0:T(8,128)}, f32[1024,1024]{1,0:T(8,128)}, f32[1024,1024]{1,0:T(8,128)}), (f32[1024,768]{1,0:T(8,128)}, f32[256,1024]{1,0:T(8,128)}, f32[1024,1024]{1,0:T(8,128)}, ...) | async-done | bytes 12582928 | tf_op jit(solution)/shard_map/psum | solution.py:129
  755.5 3.9 copy.104
  760.3 2.1 copy.106
  762.5 1.6 copy-done.15
  764.0 2.0 copy.107
  (103 shorter events, 13.3 us)
Async XLA Ops:
  7.2 172.4 %copy-start = (bf16[1024,1024]{1,0:T(8,128)(2,1)S(1)}, bf16[1024,1024]{1,0:T(8,128)(2,1)}, u32[]{:S(2)}) copy-start(bf16[1024,1024]{1,0:T(8,128)(2,1)} %param.20) | copy-start | bytes 6291460
  7.2 168.9 %all-reduce.8.cloned.1.call-start = ((), (), s32[]{:S(2)}) async-start(), calls=%async_computation | async-start | bytes 8388608 | tf_op jit(solution)/shard_map/psum | solution.py:71
  7.2 17.0 %copy-start.11 = (bf16[8192,1024]{1,0:T(8,128)(2,1)S(1)}, bf16[8192,1024]{1,0:T(8,128)(2,1)}, u32[]{:S(2)}) copy-start(bf16[8192,1024]{1,0:T(8,128)(2,1)} %param.14) | copy-start | bytes 50331652
  24.2 6.2 copy-start.27
  30.5 16.0 %copy-start.28 = (bf16[1024]{0:T(1024)(128)(2,1)S(1)}, bf16[1024]{0:T(1024)(128)(2,1)}, u32[]{:S(2)}) copy-start(bf16[1024]{0:T(1024)(128)(2,1)} %param.15) | copy-start | bytes 6148
  51.6 5.4 copy-start.25
  57.0 8.4 %copy-start.18 = (bf16[8,128,4,1,64]{1,0,4,3,2:T(8,128)(2,1)}, bf16[8,128,4,1,64]{1,0,4,3,2:T(8,128)(2,1)S(1)}, u32[]{:S(2)}) copy-start(bf16[8,128,4,1,64]{1,0,4,3,2:T(8,128)(2,1)S(1)} %get-tuple-element.32) | copy-start | bytes 1572868
  57.0 8.4 %copy-start.17 = (bf16[8,128,4,1,64]{1,0,4,3,2:T(8,128)(2,1)}, bf16[8,128,4,1,64]{1,0,4,3,2:T(8,128)(2,1)S(1)}, u32[]{:S(2)}) copy-start(bf16[8,128,4,1,64]{1,0,4,3,2:T(8,128)(2,1)S(1)} %get-tuple-element.31) | copy-start | bytes 1572868
  65.0 1.3 copy-start.9
  65.5 1.4 copy-start.24
  69.6 0.7 copy-start.29
  69.6 0.7 copy-start.26
  69.6 228.4 %all-reduce.10.cloned.1.call-start = ((), (), s32[]{:S(2)}) async-start(), calls=%async_computation.1 | async-start | bytes 8388608 | tf_op jit(solution)/shard_map/psum | solution.py:87
  179.6 2.5 copy-start.3
  179.6 3.1 copy-start.6
  179.6 3.7 copy-start.30
  183.3 5.2 copy-start.32
  188.6 1.3 copy-start.34
  194.2 301.6 %all-reduce.14.cloned.1.call-start = ((), (), s32[]{:S(2)}) async-start(), calls=%async_computation.3 | async-start | bytes 16777216 | tf_op jit(solution)/shard_map/psum | solution.py:76
  194.7 108.0 %copy-start.7 = (bf16[1024,1024]{1,0:T(8,128)(2,1)S(1)}, bf16[1024,1024]{1,0:T(8,128)(2,1)}, u32[]{:S(2)}) copy-start(bf16[1024,1024]{1,0:T(8,128)(2,1)} %gather_fusion.3) | copy-start | bytes 6291460
  298.0 4.7 copy-start.4
  298.0 5.9 copy-start.5
  305.5 1.4 copy-start.13
  306.8 5.8 copy-start.10
  312.7 2.4 copy-start.20
  314.5 1.0 copy-start.19
  316.3 3.4 copy-start.31
  318.6 1.1 copy-start.21
  323.6 1.6 copy-start.35
  323.7 431.8 %all-reduce.12.cloned.1.call-start = ((), (), s32[]{:S(2)}) async-start(), calls=%async_computation.2 | async-start | bytes 25165824 | tf_op jit(solution)/shard_map/psum | solution.py:129
  325.2 6.8 copy-start.8
  325.2 6.8 copy-start.33
  332.1 5.1 copy-start.14
  332.1 6.8 copy-start.2
  332.1 6.8 copy-start.22
  495.9 5.4 copy-start.12
  755.5 3.9 copy-start.23
  755.5 4.9 copy-start.16
  760.3 3.7 copy-start.15
  760.3 5.7 copy-start.1
Sparse Core Ops, SparseCore 0:
  69.7 106.3 all-reduce.7
  194.4 103.6 all-reduce.9
  323.8 172.0 all-reduce.13
  499.5 255.9 all-reduce.11
where the time goes:
time: 783 us; the launch traced here: 775 us
  waiting for transfers between devices  490 us (63%)
  local copies, waits for them, and re-layouts  116 us (15%)
  matrix products  66.4 us (8%)
  other arithmetic  51.8 us (7%)
  blocking collectives  31 us (4%)
  between operations  19 us (2%)
    psum x1, waiting for transfers between devices, shards(): lax.psum((grad_gain_attn, grad_gain_mlp, grad_router, grad_qkv, grad_out,...  167 us
    psum x1, waiting for transfers between devices, shards(): lax.psum(jnp.dot(hidden, w_down, preferred_element_type=jnp.float32), 'mp')  153 us
    psum x1, waiting for transfers between devices, shards(): lax.psum(jnp.dot(grad_pre, w_up.T, preferred_element_type=jnp.float32), '...  95.7 us
    psum x1, waiting for transfers between devices, shards(): lax.psum(jnp.dot(heads_out, w_out, preferred_element_type=jnp.float32), '...  74.5 us
    unnamed x81, local copies, waits for them, and re-layouts  44.3 us
    psum x1, blocking collectives, shards(): lax.psum((grad_gain_attn, grad_gain_mlp, grad_router, grad_qkv, grad_out,...  31 us
    scatter x1, other arithmetic, shards(): output = tokens.at[picks].set(updated_low)  23 us
    scatter x1, local copies, waits for them, and re-layouts, shards(): grad_tokens = cotangent.at[picks].set(grad_rows_low)  21.8 us
  transfers between devices with their start and end apart: 4, of which 4 were waited for; matrix products, arithmetic and copies ran while one was open for 15% of the time, Pallas kernels for 0%

commit v1 on v0

--- a/solution.py
+++ b/solution.py
@@ -73,7 +73,9 @@
     normed_two = rms_scale(middle, gain_two).astype(jnp.bfloat16)
     pre_act = jnp.dot(normed_two, w_up, preferred_element_type=jnp.float32)
     hidden = jax.nn.gelu(pre_act).astype(jnp.bfloat16)
-    mlp_out = lax.psum(jnp.dot(hidden, w_down, preferred_element_type=jnp.float32), "mp")
+    mlp_out = jnp.sum(
+        lax.all_gather(jnp.dot(hidden, w_down, preferred_element_type=jnp.float32), "mp"), axis=0
+    )
     delta_rows = attended + mlp_out
     updated_low = (rows_routed + rate_col * delta_rows).astype(jnp.bfloat16)
     router_term = jnp.sum(grad_rows * delta_rows, axis=-1) * rate_routed * (1.0 - rate_routed)

time: 783 us -> 883 us (1.13)
  waiting for transfers between devices: 490 us -> 570 us
  other arithmetic: 51.8 us -> 62.9 us
  starting transfers between devices: 0.95 us -> 11.9 us
    all_gather x0 -> x1, waiting for transfers between devices: none -> 155 us  [shards(): lax.all_gather(jnp.dot(hidden, w_down, preferred_element_type=jnp.float32...]
    psum x1, waiting for transfers between devices: 153 us -> 61.1 us  [shards(): lax.psum(jnp.dot(grad_joint, w_qkv.T, preferred_element_type=jnp.float32)...]
    psum x1, waiting for transfers between devices: 167 us -> 194 us  [shards(): lax.psum((grad_gain_attn, grad_gain_mlp, grad_router, grad_qkv, grad_out,...]
    psum x1, starting transfers between devices: 0.25 us -> 11.1 us  [shards(): lax.psum(jnp.dot(grad_pre, w_up.T, preferred_element_type=jnp.float32), '...]
    psum x1, waiting for transfers between devices: 74.5 us -> 63.9 us  [shards(): lax.psum(jnp.dot(heads_out, w_out, preferred_element_type=jnp.float32), '...]
    reduce_sum x0 -> x1, other arithmetic: none -> 10.5 us  [shards(): jnp.sum(lax.all_gather(jnp.dot(hidden, w_down, preferred_element_type=jnp...]
  transfers between devices with their start and end apart: 4 -> 5, of which waited for: 4 -> 5; matrix products, arithmetic and copies ran while one was open for 15% -> 13% of each run, Pallas kernels for 0% -> 0%
where the time goes in v1:
time: 883 us; the launch traced here: 876 us
  waiting for transfers between devices  570 us (65%)
  local copies, waits for them, and re-layouts  116 us (13%)
  matrix products  65.7 us (7%)
  other arithmetic  62.9 us (7%)
  blocking collectives  31 us (4%)
  between operations  18.9 us (2%)
  starting transfers between devices  11.9 us (1%)
    psum x1, waiting for transfers between devices, shards(): lax.psum((grad_gain_attn, grad_gain_mlp, grad_router, grad_qkv, grad_out,...  194 us
    all_gather x1, waiting for transfers between devices, shards(): lax.all_gather(jnp.dot(hidden, w_down, preferred_element_type=jnp.float32...  155 us
    psum x1, waiting for transfers between devices, shards(): lax.psum(jnp.dot(grad_pre, w_up.T, preferred_element_type=jnp.float32), '...  94.9 us
    psum x1, waiting for transfers between devices, shards(): lax.psum(jnp.dot(heads_out, w_out, preferred_element_type=jnp.float32), '...  63.9 us
    psum x1, waiting for transfers between devices, shards(): lax.psum(jnp.dot(grad_joint, w_qkv.T, preferred_element_type=jnp.float32)...  61.1 us
    unnamed x81, local copies, waits for them, and re-layouts  44.5 us
    psum x1, blocking collectives, shards(): lax.psum((grad_gain_attn, grad_gain_mlp, grad_router, grad_qkv, grad_out,...  31 us
    scatter x1, other arithmetic, shards(): output = tokens.at[picks].set(updated_low)  23.1 us
  transfers between devices with their start and end apart: 5, of which 5 were waited for; matrix products, arithmetic and copies ran while one was open for 13% of the time, Pallas kernels for 0%

profile of v1, /device:TPU:0, one launch (start us, length us, event | category | flops | bytes accessed | tf_op | source)
XLA Modules:
  0.0 875.8 jit_solution(3794728271205063168)
XLA Ops:
  7.3 14.9 %copy.101 = bf16[8192,1024]{1,0:T(8,128)(2,1)} copy(bf16[8192,1024]{1,0:T(8,128)(2,1)} %param.11) | data formatting | bytes 33554432
  22.2 2.1 copy-done.11
  24.3 6.2 copy.102
  30.6 13.9 %gather_fusion = bf16[1024,1024]{1,0:T(8,128)(2,1)} fusion(bf16[8192,1024]{1,0:T(8,128)(2,1)} %copy.101, s32[1024]{0:T(1024)S(1)} %broadcast_clamp_fusion), kind=kCustom, calls=%fused_computation | custom fusion | bytes 4198400 | tf_op jit(solution)/shard_map/gather | solution.py:36
  44.5 2.1 fusion.18
  46.6 5.0 convolution_convert_fusion
  51.6 2.6 copy.31
  54.2 1.8 copy.53
  57.0 6.2 gather_fusion.2
  63.4 1.6 fusion.65
  66.8 2.8 fusion.52
  69.6 11.1 %all-reduce.9.cloned.1.call-start = ((), (), s32[]{:S(2)}) async-start(), calls=%async_computation.1 | async-start | bytes 8388608 | tf_op jit(solution)/shard_map/psum | solution.py:89
  80.7 10.5 %fusion.66 = f32[1,8192]{1,0:T(1,128)S(1)} fusion(bf16[8192,1024]{1,0:T(8,128)(2,1)} %copy.101, bf16[1024,1]{0,1:T(2,128)(2,1)S(1)} %reshape.201), kind=kOutput, calls=%fused_computation.113 | convolution fusion | flops 16777216 | bytes 16812032 | tf_op jit(solution)/shard_map/dot_general | solution.py:30
  91.8 6.1 gather_fusion.1
  98.0 14.1 %gather_fusion.3 = bf16[1024,1024]{1,0:T(8,128)(2,1)} fusion(bf16[8192,1024]{1,0:T(8,128)(2,1)} %copy.102, s32[1024]{0:T(1024)S(1)} %broadcast_clamp_fusion), kind=kCustom, calls=%fused_computation.3 | custom fusion | bytes 4198400 | tf_op jit(solution)/shard_map/gather | solution.py:37
  112.1 63.9 %all-reduce.7.cloned.1.call-done = f32[1024,1024]{1,0:T(8,128)} async-done(((f32[1024,1024]{1,0:T(8,128)}), f32[1024,1024]{1,0:T(8,128)}) %all-reduce.7.cloned.1.call-update) | async-done | bytes 4194320 | tf_op jit(solution)/shard_map/psum | solution.py:71
  176.1 3.5 multiply_reduce_fusion.2
  179.6 2.4 fusion.60
  183.3 5.2 fusion.13
  189.9 4.3 fusion.67
  194.3 1.5 copy-done.30
  195.8 6.8 fusion.61
  203.1 94.9 %all-reduce.9.cloned.1.call-done = f32[1024,1024]{1,0:T(8,128)} async-done(((f32[1024,1024]{1,0:T(8,128)}), f32[1024,1024]{1,0:T(8,128)}) %all-reduce.9.cloned.1.call-update) | async-done | bytes 4194320 | tf_op jit(solution)/shard_map/psum | solution.py:89
  298.0 4.5 multiply_reduce_fusion
  302.5 155.2 %all-gather.3.cloned.1.call-done = f32[4096,1024]{1,0:T(8,128)} async-done(((f32[1024,1024]{1,0:T(8,128)}), f32[4096,1024]{1,0:T(8,128)}) %all-gather.3.cloned.1.call-update) | async-done | bytes 16777232 | tf_op jit(solution)/shard_map/all_gather | solution.py:77
  457.7 10.5 %reduce_sum.119 = f32[1024,1024]{1,0:T(8,128)} reduce(f32[4,1024,1024]{2,1,0:T(8,128)} %bitcast.86, f32[]{:T(128)} %constant.8.clone.1), dimensions={0}, to_apply=%region_5.6 | reduce | flops 3145728 | bytes 20971524 | tf_op jit(solution)/shard_map/reduce_sum | solution.py:76
  468.2 7.0 fusion.17
  475.2 1.4 copy-done.12
  476.6 1.6 convolution_convert_fusion.2
  478.1 2.8 reshape.203
  480.9 1.5 copy.38
  483.3 1.8 multiply_reduce_fusion.3
  489.5 3.8 fusion.30
  494.9 6.8 fusion.59
  501.7 5.1 fusion.42
  506.8 1.7 fusion.50
  508.5 3.8 fusion.28
  512.3 23.1 %scatter_custom_fusion = bf16[8192,1024]{1,0:T(8,128)(2,1)} fusion(bf16[8192,1024]{1,0:T(8,128)(2,1)} %copy.101, s32[1024]{0:T(1024)S(1)} %bitcast.100, bf16[1024,1024]{1,0:T(8,128)(2,1)S(1)} %copy-done.2, f32[1024]{0:T(1024)S(1)} %gather_fusion.1, f32[1024,1024]{1,0:T(8,128)} %all-reduce.7.cloned.1.call-done, f32[1024,1024]{1,0:T(8,128)} %reduce_sum.119), kind=kCustom, calls=%fused_computation.47 | custom fusion | flops 5242880 | bytes 27267072 | tf_op jit(solution)/shard_map/scatter | solution.py:82
  536.0 61.1 %all-reduce.11.cloned.1.call-done = f32[1024,1024]{1,0:T(8,128)} async-done(((f32[1024,1024]{1,0:T(8,128)}), f32[1024,1024]{1,0:T(8,128)}) %all-reduce.11.cloned.1.call-update) | async-done | bytes 4194320 | tf_op jit(solution)/shard_map/psum | solution.py:120
  597.1 3.8 fusion.5
  601.2 5.8 fusion.16
  607.0 21.6 %scatter_fusion = bf16[8192,1024]{1,0:T(8,128)(2,1)} fusion(bf16[8192,1024]{1,0:T(8,128)(2,1)} %copy.102, s32[1024]{0:T(1024)S(1)} %bitcast.101, bf16[1024,1024]{1,0:T(8,128)(2,1)} %fusion.16), kind=kCustom, calls=%fused_computation.5 | custom fusion | bytes 6295552 | tf_op jit(solution)/shard_map/scatter | solution.py:130
  628.5 31.0 %all-reduce = (f32[1024]{0:T(1024)}, f32[1024]{0:T(1024)}, f32[1024]{0:T(1024)}, f32[]{:T(128)}, f32[]{:T(128)}) all-reduce(f32[1024]{0:T(1024)S(1)} %get-tuple-element.13, f32[1024]{0:T(1024)S(1)} %get-tuple-element.11, f32[1024]{0:T(1024)S(1)} %get-tuple-element.15, f32[]{:T(128)} %get-tuple-element.34, ...), channel_id=1, replica_groups=mesh['dp'=8,'mp'=4] {'dp'}, use_global_device_ids=true, to_apply=%region_15.16 | all-reduce | flops 3074 | bytes 24592 | tf_op jit(solution)/shard_map/psum | solution.py:131
  661.5 194.5 %all-reduce.13.cloned.1.call-done = (f32[1024,768]{1,0:T(8,128)}, f32[256,1024]{1,0:T(8,128)}, f32[1024,1024]{1,0:T(8,128)}, f32[1024,1024]{1,0:T(8,128)}) async-done(((f32[1024,768]{1,0:T(8,128)}, f32[256,1024]{1,0:T(8,128)}, f32[1024,1024]{1,0:T(8,128)}, f32[1024,1024]{1,0:T(8,128)}), (f32[1024,768]{1,0:T(8,128)}, f32[256,1024]{1,0:T(8,128)}, f32[1024,1024]{1,0:T(8,128)}, ...) | async-done | bytes 12582928 | tf_op jit(solution)/shard_map/psum | solution.py:131
  856.0 3.9 copy.103
  860.9 2.1 copy.105
  863.0 1.6 copy-done.14
  864.6 2.0 copy.106
  (106 shorter events, 15.7 us)
Async XLA Ops:
  7.2 172.4 %copy-start = (bf16[1024,1024]{1,0:T(8,128)(2,1)S(1)}, bf16[1024,1024]{1,0:T(8,128)(2,1)}, u32[]{:S(2)}) copy-start(bf16[1024,1024]{1,0:T(8,128)(2,1)} %param.20) | copy-start | bytes 6291460
  7.2 168.9 %all-reduce.7.cloned.1.call-start = ((), (), s32[]{:S(2)}) async-start(), calls=%async_computation | async-start | bytes 8388608 | tf_op jit(solution)/shard_map/psum | solution.py:71
  7.2 17.0 %copy-start.11 = (bf16[8192,1024]{1,0:T(8,128)(2,1)S(1)}, bf16[8192,1024]{1,0:T(8,128)(2,1)}, u32[]{:S(2)}) copy-start(bf16[8192,1024]{1,0:T(8,128)(2,1)} %param.14) | copy-start | bytes 50331652
  24.2 6.2 copy-start.26
  24.3 6.3 copy-start.27
  51.6 5.4 copy-start.24
  57.0 8.4 copy-start.17
  57.0 8.4 copy-start.16
  65.0 1.3 copy-start.5
  65.4 1.4 copy-start.23
  69.5 11.2 %copy-start.25 = (bf16[1024]{0:T(1024)(128)(2,1)S(1)}, bf16[1024]{0:T(1024)(128)(2,1)}, u32[]{:S(2)}) copy-start(bf16[1024]{0:T(1024)(128)(2,1)} %param.17) | copy-start | bytes 6148
  69.6 228.4 %all-reduce.9.cloned.1.call-start = ((), (), s32[]{:S(2)}) async-start(), calls=%async_computation.1 | async-start | bytes 8388608 | tf_op jit(solution)/shard_map/psum | solution.py:89
  91.2 6.8 copy-start.28
  179.5 2.5 copy-start.3
  179.6 3.1 copy-start.7
  179.6 3.7 copy-start.29
  183.3 5.2 copy-start.32
  188.5 1.3 copy-start.34
  194.2 1.6 copy-start.30
  194.2 263.5 %all-gather.3.cloned.1.call-start = ((), (), s32[]{:S(2)}) async-start(), calls=%async_computation.3 | async-start | bytes 20971520 | tf_op jit(solution)/shard_map/all_gather | solution.py:77
  202.6 394.4 %all-reduce.11.cloned.1.call-start = ((), (), s32[]{:S(2)}) async-start(), calls=%async_computation.2 | async-start | bytes 8388608 | tf_op jit(solution)/shard_map/psum | solution.py:120
  457.7 10.5 %copy-start.8 = (bf16[1024,1024]{1,0:T(8,128)(2,1)S(1)}, bf16[1024,1024]{1,0:T(8,128)(2,1)}, u32[]{:S(2)}) copy-start(bf16[1024,1024]{1,0:T(8,128)(2,1)} %gather_fusion.3) | copy-start | bytes 6291460
  475.2 1.4 copy-start.12
  476.6 5.8 copy-start.6
  483.2 2.4 copy-start.19
  485.0 1.4 copy-start.18
  486.5 3.0 copy-start.31
  488.3 1.2 copy-start.20
  493.3 1.6 copy-start.35
  493.3 362.7 %all-reduce.13.cloned.1.call-start = ((), (), s32[]{:S(2)}) async-start(), calls=%async_computation.4 | async-start | bytes 25165824 | tf_op jit(solution)/shard_map/psum | solution.py:131
  494.9 6.8 copy-start.9
  494.9 6.8 copy-start.33
  501.7 5.1 copy-start.13
  501.7 6.8 copy-start.2
  501.7 6.8 copy-start.21
  597.1 3.8 copy-start.4
  597.1 4.1 copy-start.10
  856.0 3.9 copy-start.22
  856.0 4.9 copy-start.15
  860.9 3.7 copy-start.14
  860.9 5.7 copy-start.1
Sparse Core Ops, SparseCore 0:
  69.7 106.3 all-reduce.6
  194.3 103.5 all-reduce.8
  300.4 157.2 all-gather.2
  493.4 103.5 all-reduce.10
  600.7 255.2 all-reduce.12
